TPU v7x, 32 devices: a whole 2x2x4 slice. The times are simulated.
32 devices in a mesh: wide: 8 (over y, x, core), narrow: 4 (over z).
Axes of the slice: x: 2, y: 2, z: 4, core: 2. Of those that a mesh axis runs over, the one named last changes fastest.
Arguments:
- vectors: bfloat16 [3, 4096, 128], P(None, ('wide', 'narrow')), may hold values from -18 to 18
- hessian: bfloat16 [3, 3, 61, 4096], P(None, None, None, ('wide', 'narrow')), may hold values from -0.9 to 5.4
- neighbours: int32 [60, 4096], P(None, ('wide', 'narrow')), may hold values from 0 to 415
- halo_atoms: int32 [1024], P(('wide', 'narrow')), may hold values from 0 to 127
- labels: int32 [4096], P(('wide', 'narrow')), may hold values from 0 to 15
- masses: float32 [2, 16], replicated, may hold values from 1 to 32
- rotation: float32 [2, 128, 128], replicated, may hold values from -0.5 to 0.5
Outputs:
- gram: float32 [2, 128, 128], replicated
- rotated: bfloat16 [2, 3, 4096, 128], P(None, None, ('wide', 'narrow'))
Inputs may be any that keep to these rules, and one draw needn't show every extreme that they name: `neighbours`: A row below 128 is a local atom of the domain; a row r at or above it is boundary atom (r - 128) % 32 of block (r - 128) // 32 in the 3x3 order of the steps.
All inputs are finite; a program needn't handle non-finite values.
Results may differ from a plain program's by a relative error of at most 0.003.
Values may be sent and summed in bfloat16 or wider, within the bound.
No kernel may reach another device: no remote copies, remote signals or barrier semaphores. Data moves between devices by JAX's collectives and lax.ppermute only.
A program may use at most 64 MiB of HBM per device.

v0:
```python
import jax
import jax.numpy as jnp
from jax import lax
from jax.sharding import PartitionSpec as P


def padded(array, sides, width):
    for axis, dim in sides:
        size, length = (lax.axis_size(axis), array.shape[dim])
        up = [(i, (i + 1) % size) for i in range(size - 1)]
        down = [(j, i) for i, j in up]
        last = lax.slice_in_dim(array, length - width, length, axis=dim)
        leading = lax.slice_in_dim(array, 0, width, axis=dim)
        before = lax.ppermute(last, axis, up)
        after = lax.ppermute(leading, axis, down)
        array = jnp.concatenate([before, array, after], axis=dim)
    return array


def class_factors(inverse_roots, classes):
    onehot = (
        classes[None, :] == jnp.arange(inverse_roots.shape[1], dtype=jnp.int32)[:, None]
    ).astype(jnp.float32)
    return jnp.dot(inverse_roots, onehot, precision=lax.Precision.HIGHEST)


def scale_rows(rows_full, factors):
    return jnp.concatenate(
        [rows_full * factors[0][None, :, None], rows_full * factors[1][None, :, None]], axis=2
    ).astype(jnp.bfloat16)


def local(vectors, hessian, neighbours, halo_atoms, labels, masses, rotation):
    atoms_here = vectors.shape[1]
    width = vectors.shape[2]
    boundary = halo_atoms.shape[0]
    inverse_roots = lax.rsqrt(masses)
    factors = class_factors(inverse_roots, labels)
    vector_complete = vectors.astype(jnp.float32)
    scaled = scale_rows(vector_complete, factors)
    outgoing = jnp.take(scaled, halo_atoms, axis=1)[:, None, None]
    rims = padded(outgoing, (("wide", 1), ("narrow", 2)), 1)
    rim_rows = rims.reshape(3, 9 * boundary, 2 * width)
    extended = jnp.concatenate([scaled, rim_rows], axis=1)
    total = jnp.einsum("ija,jac->iac", hessian[:, :, 0], scaled, preferred_element_type=jnp.float32)

    def add_group(group, running):
        blocks = lax.dynamic_slice_in_dim(hessian, 1 + group * 4, 4, 2)
        indices = lax.dynamic_slice_in_dim(neighbours, group * 4, 4, 0)
        picked = jnp.take(extended, indices.reshape(-1), axis=1).reshape(
            3, 4, atoms_here, 2 * width
        )
        return running + jnp.einsum(
            "ijka,jkac->iac", blocks, picked, preferred_element_type=jnp.float32
        )

    total = lax.fori_loop(0, neighbours.shape[0] // 4, add_group, total)
    hydrogen_image = total[:, :, :width] * factors[0][None, :, None]
    deuterium_image = total[:, :, width:] * factors[1][None, :, None]
    partial_gram = jnp.stack(
        [
            jnp.einsum(
                "eqv,eqh->vh", vector_complete, hydrogen_image, precision=lax.Precision.HIGHEST
            ),
            jnp.einsum(
                "eqv,eqh->vh", vector_complete, deuterium_image, precision=lax.Precision.HIGHEST
            ),
        ]
    )
    atoms_all = 3.0 * atoms_here * lax.axis_size("wide") * lax.axis_size("narrow")
    images = (hydrogen_image, deuterium_image)
    gram = lax.psum(partial_gram, ("wide", "narrow")) / atoms_all
    outputs = []
    for isotope_variant in range(2):
        fresh_block = images[isotope_variant] - jnp.einsum(
            "jyx,xs->jys", vector_complete, gram[isotope_variant], precision=lax.Precision.HIGHEST
        )
        outputs.append(
            jnp.einsum(
                "jyx,xs->jys",
                fresh_block,
                rotation[isotope_variant],
                precision=lax.Precision.HIGHEST,
            ).astype(jnp.bfloat16)
        )
    return (gram, jnp.stack(outputs))


def solution(mesh):
    return jax.shard_map(
        local,
        mesh=mesh,
        in_specs=(
            P(None, ("wide", "narrow"), None),
            P(None, None, None, ("wide", "narrow")),
            P(None, ("wide", "narrow")),
            P(("wide", "narrow")),
            P(("wide", "narrow")),
            P(),
            P(),
        ),
        out_specs=(P(), P(None, None, ("wide", "narrow"), None)),
        check_vma=False,
    )
```

profile of v0, /device:TPU:0, one launch (start us, length us, event | category | flops | bytes accessed | tf_op | source)
XLA Modules:
  0.0 256.7 jit_solution(16522191547537341307)
XLA Ops:
  12.6 3.0 %collective-permute-start = (bf16[3,1,1,32,256]{4,0,3,2,1:T(4,128)(2,1)S(1)}, bf16[3,1,1,32,256]{4,0,3,2,1:T(4,128)(2,1)S(1)}, u32[]{:S(2)}, u32[]{:S(2)}) collective-permute-start(bf16[3,1,1,32,256]{4,0,3,2,1:T(4,128)(2,1)S(1)} %bitcast_select_fusion), channel_id=1, source_target_pairs={{0,4},{4,8},{8,12},{12,16},{16,20},{20,24},{24,28},{1,5},{5,9},{9,... | collective-permute-start | bytes 147464 | tf_op jit(solution)/shard_map/ppermute | solution.py:14
  18.1 5.6 %collective-permute-start.2 = (bf16[3,3,1,32,256]{4,0,3,2,1:T(4,128)(2,1)S(1)}, bf16[3,3,1,32,256]{4,0,3,2,1:T(4,128)(2,1)S(1)}, u32[]{:S(2)}, u32[]{:S(2)}) collective-permute-start(bf16[3,3,1,32,256]{4,0,3,2,1:T(4,128)(2,1)S(1)} %pad_maximum_fusion.3), channel_id=1, source_target_pairs={{0,1},{1,2},{2,3},{4,5},{5,6},{6,7},{8,9},{9,10},{10,11},{12,13},{... | collective-permute-start | bytes 442376 | tf_op jit(solution)/shard_map/ppermute | solution.py:14
  24.0 2.6 %collective-permute-done.3 = bf16[3,3,1,32,256]{4,0,3,2,1:T(4,128)(2,1)S(1)} collective-permute-done((bf16[3,3,1,32,256]{4,0,3,2,1:T(4,128)(2,1)S(1)}, bf16[3,3,1,32,256]{4,0,3,2,1:T(4,128)(2,1)S(1)}, u32[]{:S(2)}, u32[]{:S(2)}) %collective-permute-start.3) | collective-permute-done | bytes 147488 | tf_op jit(solution)/shard_map/ppermute | solution.py:15
  26.5 1.7 collective-permute-done.2
  29.5 86.3 %while.15 = (s32[]{:T(128)}, f32[3,128,256]{2,0,1:T(4,128)S(1)}, s32[60,128]{1,0:T(8,128)}, bf16[3,416,256]{2,0,1:T(4,128)(2,1)S(1)}, bf16[3,3,61,128]{3,2,1,0:T...) while((s32[]{:T(128)}, f32[3,128,256]{2,0,1:T(4,128)S(1)}, ...), condition=%wide.region_1.2_spmd, body=%wide.region_0.1_spmd.sunk | while | flops 2856458 | bytes 3210441 | solution.py:57
  31.5 2.4 gather_fusion
  33.9 1.4 fusion.30
  37.2 2.4 gather_fusion
  39.6 1.4 fusion.30
  43.0 2.4 gather_fusion
  45.4 1.4 fusion.30
  48.7 2.4 gather_fusion
  51.1 1.4 fusion.30
  54.5 2.4 gather_fusion
  56.9 1.4 fusion.30
  60.2 2.4 gather_fusion
  62.7 1.4 fusion.30
  66.0 2.4 gather_fusion
  68.4 1.4 fusion.30
  71.8 2.4 gather_fusion
  74.2 1.4 fusion.30
  77.5 2.4 gather_fusion
  79.9 1.4 fusion.30
  83.3 2.4 gather_fusion
  85.7 1.4 fusion.30
  89.0 2.4 gather_fusion
  94.8 2.4 gather_fusion
  100.5 2.4 gather_fusion
  106.3 2.4 gather_fusion
  108.7 1.4 fusion.30
  112.0 2.4 gather_fusion
  117.4 128.9 %all-reduce.2.cloned.1.call-done = f32[2,128,128]{1,2,0:T(8,128)} async-done(((f32[2,128,128]{1,2,0:T(8,128)}), f32[2,128,128]{1,2,0:T(8,128)}) %all-reduce.2.cloned.1.call-update) | async-done | bytes 131088 | tf_op jit(solution)/shard_map/psum | solution.py:72
  (133 shorter events, 48.5 us)
Async XLA Ops:
  7.2 239.1 %all-reduce.2.cloned.1.call-start = ((), (), s32[]{:S(2)}) async-start(), calls=%async_computation | async-start | bytes 262144 | tf_op jit(solution)/shard_map/psum | solution.py:72
  11.3 5.3 %collective-permute-start.1 = (bf16[3,1,1,32,256]{4,0,3,2,1:T(4,128)(2,1)S(1)}, bf16[3,1,1,32,256]{4,0,3,2,1:T(4,128)(2,1)S(1)}, u32[]{:S(2)}, u32[]{:S(2)}) collective-permute-start(bf16[3,1,1,32,256]{4,0,3,2,1:T(4,128)(2,1)S(1)} %bitcast_select_fusion), channel_id=1, source_target_pairs={{4,0},{8,4},{12,8},{16,12},{20,16},{24,20},{28,24},{5,1},{9,5},{13... | collective-permute-start | bytes 147464 | tf_op jit(solution)/shard_map/ppermute | solution.py:15
  12.6 4.0 %collective-permute-start = (bf16[3,1,1,32,256]{4,0,3,2,1:T(4,128)(2,1)S(1)}, bf16[3,1,1,32,256]{4,0,3,2,1:T(4,128)(2,1)S(1)}, u32[]{:S(2)}, u32[]{:S(2)}) collective-permute-start(bf16[3,1,1,32,256]{4,0,3,2,1:T(4,128)(2,1)S(1)} %bitcast_select_fusion), channel_id=1, source_target_pairs={{0,4},{4,8},{8,12},{12,16},{16,20},{20,24},{24,28},{1,5},{5,9},{9,... | collective-permute-start | bytes 147464 | tf_op jit(solution)/shard_map/ppermute | solution.py:14
  16.8 9.8 %collective-permute-start.3 = (bf16[3,3,1,32,256]{4,0,3,2,1:T(4,128)(2,1)S(1)}, bf16[3,3,1,32,256]{4,0,3,2,1:T(4,128)(2,1)S(1)}, u32[]{:S(2)}, u32[]{:S(2)}) collective-permute-start(bf16[3,3,1,32,256]{4,0,3,2,1:T(4,128)(2,1)S(1)} %pad_maximum_fusion.3), channel_id=1, source_target_pairs={{1,0},{2,1},{3,2},{5,4},{6,5},{7,6},{9,8},{10,9},{11,10},{13,12},{... | collective-permute-start | bytes 442376 | tf_op jit(solution)/shard_map/ppermute | solution.py:15
  18.1 10.2 %collective-permute-start.2 = (bf16[3,3,1,32,256]{4,0,3,2,1:T(4,128)(2,1)S(1)}, bf16[3,3,1,32,256]{4,0,3,2,1:T(4,128)(2,1)S(1)}, u32[]{:S(2)}, u32[]{:S(2)}) collective-permute-start(bf16[3,3,1,32,256]{4,0,3,2,1:T(4,128)(2,1)S(1)} %pad_maximum_fusion.3), channel_id=1, source_target_pairs={{0,1},{1,2},{2,3},{4,5},{5,6},{6,7},{8,9},{9,10},{10,11},{12,13},{... | collective-permute-start | bytes 442376 | tf_op jit(solution)/shard_map/ppermute | solution.py:14
  29.5 86.4 %copy-start = (bf16[3,128,128]{2,1,0:T(8,128)(2,1)S(1)}, bf16[3,128,128]{2,1,0:T(8,128)(2,1)}, u32[]{:S(2)}) copy-start(bf16[3,128,128]{2,1,0:T(8,128)(2,1)} %param.9) | copy-start | bytes 294916
  116.7 131.8 %copy-start.1 = (f32[2,128,128]{2,1,0:T(8,128)S(1)}, f32[2,128,128]{2,1,0:T(8,128)}, u32[]{:S(2)}) copy-start(f32[2,128,128]{2,1,0:T(8,128)} %param.15) | copy-start | bytes 393220
Sparse Core Ops, SparseCore 0:
  117.5 128.6 all-reduce.1
where the time goes:
time: 258 us; the launch traced here: 257 us
  waiting for transfers between devices  133 us (52%)
  local copies, waits for them, and re-layouts  56.9 us (22%)
  matrix products  24.1 us (9%)
  other arithmetic  16.2 us (6%)
  between operations  14.2 us (6%)
  starting transfers between devices  11.3 us (4%)
    psum x1, waiting for transfers between devices, local(): gram = lax.psum(partial_gram, ('wide', 'narrow')) / atoms_all  129 us
    gather x15, local copies, waits for them, and re-layouts, add_group(): jnp.take(extended, indices.reshape(-1), axis=1)  36 us
    dot_general x15, matrix products, add_group(): jnp.einsum('ijka,jkac->iac', blocks, picked, preferred_element_type=jnp.f...  21.1 us
    dynamic_slice x30, local copies, waits for them, and re-layouts, add_group(): blocks = lax.dynamic_slice_in_dim(hessian, 1 + group * 4, 4, 2)  15.7 us
    and x15, other arithmetic, add_group(): jnp.take(extended, indices.reshape(-1), axis=1)  10.6 us
    ppermute x2, starting transfers between devices, padded(): before = lax.ppermute(last, axis, up)  8.63 us
  transfers between devices with their start and end apart: 5, of which 3 were waited for; matrix products, arithmetic and copies ran while one was open for 0% of the time, Pallas kernels for 0%

commit v1 on v0

--- a/solution.py
+++ b/solution.py
@@ -2,6 +2,12 @@
 import jax.numpy as jnp
 from jax import lax
 from jax.sharding import PartitionSpec as P
+
+
+def gather_and_add(shard, axis):
+    shards = lax.all_gather(shard, axis, axis=0, tiled=False)
+    total = shards.sum(axis=0)
+    return total
 
 
 def padded(array, sides, width):
@@ -69,7 +75,7 @@
     )
     atoms_all = 3.0 * atoms_here * lax.axis_size("wide") * lax.axis_size("narrow")
     images = (hydrogen_image, deuterium_image)
-    gram = lax.psum(partial_gram, ("wide", "narrow")) / atoms_all
+    gram = gather_and_add(partial_gram, ("wide", "narrow")) / atoms_all
     outputs = []
     for isotope_variant in range(2):
         fresh_block = images[isotope_variant] - jnp.einsum(

time: 258 us -> 196 us (0.76)
  waiting for transfers between devices: 133 us -> 70.3 us
    psum x1 -> x0, waiting for transfers between devices: 129 us -> none  [local(): gram = lax.psum(partial_gram, ('wide', 'narrow')) / atoms_all]
    all_gather x0 -> x1, waiting for transfers between devices: none -> 66 us  [gather_and_add(): shards = lax.all_gather(shard, axis, axis=0, tiled=False)]
  transfers between devices with their start and end apart: 5 -> 5, of which waited for: 3 -> 3; matrix products, arithmetic and copies ran while one was open for 0% -> 1% of each run, Pallas kernels for 0% -> 0%
where the time goes in v1:
time: 196 us; the launch traced here: 195 us
  waiting for transfers between devices  70.3 us (36%)
  local copies, waits for them, and re-layouts  57.8 us (29%)
  matrix products  23.2 us (12%)
  other arithmetic  17 us (9%)
  between operations  14.3 us (7%)
  starting transfers between devices  11.3 us (6%)
    all_gather x1, waiting for transfers between devices, gather_and_add(): shards = lax.all_gather(shard, axis, axis=0, tiled=False)  66 us
    gather x15, local copies, waits for them, and re-layouts, add_group(): jnp.take(extended, indices.reshape(-1), axis=1)  36 us
    dot_general x15, matrix products, add_group(): jnp.einsum('ijka,jkac->iac', blocks, picked, preferred_element_type=jnp.f...  20.2 us
    dynamic_slice x30, local copies, waits for them, and re-layouts, add_group(): blocks = lax.dynamic_slice_in_dim(hessian, 1 + group * 4, 4, 2)  15.7 us
    and x15, other arithmetic, add_group(): jnp.take(extended, indices.reshape(-1), axis=1)  10.6 us
    ppermute x2, starting transfers between devices, padded(): before = lax.ppermute(last, axis, up)  8.63 us
  transfers between devices with their start and end apart: 5, of which 3 were waited for; matrix products, arithmetic and copies ran while one was open for 1% of the time, Pallas kernels for 0%

profile of v1, /device:TPU:0, one launch (start us, length us, event | category | flops | bytes accessed | tf_op | source)
XLA Modules:
  0.0 194.7 jit_solution(9379338001247940526)
XLA Ops:
  12.6 3.0 %collective-permute-start = (bf16[3,1,1,32,256]{4,0,3,2,1:T(4,128)(2,1)S(1)}, bf16[3,1,1,32,256]{4,0,3,2,1:T(4,128)(2,1)S(1)}, u32[]{:S(2)}, u32[]{:S(2)}) collective-permute-start(bf16[3,1,1,32,256]{4,0,3,2,1:T(4,128)(2,1)S(1)} %bitcast_select_fusion), channel_id=1, source_target_pairs={{0,4},{4,8},{8,12},{12,16},{16,20},{20,24},{24,28},{1,5},{5,9},{9,... | collective-permute-start | bytes 147464 | tf_op jit(solution)/shard_map/ppermute | solution.py:20
  18.1 5.6 %collective-permute-start.2 = (bf16[3,3,1,32,256]{4,0,3,2,1:T(4,128)(2,1)S(1)}, bf16[3,3,1,32,256]{4,0,3,2,1:T(4,128)(2,1)S(1)}, u32[]{:S(2)}, u32[]{:S(2)}) collective-permute-start(bf16[3,3,1,32,256]{4,0,3,2,1:T(4,128)(2,1)S(1)} %pad_maximum_fusion.3), channel_id=1, source_target_pairs={{0,1},{1,2},{2,3},{4,5},{5,6},{6,7},{8,9},{9,10},{10,11},{12,13},{... | collective-permute-start | bytes 442376 | tf_op jit(solution)/shard_map/ppermute | solution.py:20
  24.0 2.6 %collective-permute-done.3 = bf16[3,3,1,32,256]{4,0,3,2,1:T(4,128)(2,1)S(1)} collective-permute-done((bf16[3,3,1,32,256]{4,0,3,2,1:T(4,128)(2,1)S(1)}, bf16[3,3,1,32,256]{4,0,3,2,1:T(4,128)(2,1)S(1)}, u32[]{:S(2)}, u32[]{:S(2)}) %collective-permute-start.3) | collective-permute-done | bytes 147488 | tf_op jit(solution)/shard_map/ppermute | solution.py:21
  26.5 1.7 collective-permute-done.2
  29.5 85.4 %while.15 = (s32[]{:T(128)}, f32[3,128,256]{2,0,1:T(4,128)S(1)}, s32[60,128]{1,0:T(8,128)}, bf16[3,416,256]{2,0,1:T(4,128)(2,1)S(1)}, bf16[3,3,61,128]{3,2,1,0:T...) while((s32[]{:T(128)}, f32[3,128,256]{2,0,1:T(4,128)S(1)}, ...), condition=%wide.region_1.2_spmd, body=%wide.region_0.1_spmd.sunk | while | flops 2856458 | bytes 3210441 | solution.py:63
  31.5 2.4 %gather_fusion = bf16[512,3,256]{2,1,0:T(4,128)(2,1)S(1)} fusion(bf16[3,416,256]{2,0,1:T(4,128)(2,1)S(1)} %get-tuple-element.240, s32[1024]{0:T(1024)S(1)} %pad_clamp_fusion.3), kind=kCustom, calls=%fused_computation.clone.1 | custom fusion | bytes 1574912 | tf_op jit(solution)/shard_map/while/body/eval_jaxpr/jit(_take)/gather | solution.py:56
  33.9 1.3 fusion.30
  37.2 2.4 %gather_fusion = bf16[512,3,256]{2,1,0:T(4,128)(2,1)S(1)} fusion(bf16[3,416,256]{2,0,1:T(4,128)(2,1)S(1)} %get-tuple-element.240, s32[1024]{0:T(1024)S(1)} %pad_clamp_fusion.3), kind=kCustom, calls=%fused_computation.clone.1 | custom fusion | bytes 1574912 | tf_op jit(solution)/shard_map/while/body/eval_jaxpr/jit(_take)/gather | solution.py:56
  39.6 1.3 fusion.30
  42.9 2.4 %gather_fusion = bf16[512,3,256]{2,1,0:T(4,128)(2,1)S(1)} fusion(bf16[3,416,256]{2,0,1:T(4,128)(2,1)S(1)} %get-tuple-element.240, s32[1024]{0:T(1024)S(1)} %pad_clamp_fusion.3), kind=kCustom, calls=%fused_computation.clone.1 | custom fusion | bytes 1574912 | tf_op jit(solution)/shard_map/while/body/eval_jaxpr/jit(_take)/gather | solution.py:56
  45.3 1.3 fusion.30
  48.6 2.4 %gather_fusion = bf16[512,3,256]{2,1,0:T(4,128)(2,1)S(1)} fusion(bf16[3,416,256]{2,0,1:T(4,128)(2,1)S(1)} %get-tuple-element.240, s32[1024]{0:T(1024)S(1)} %pad_clamp_fusion.3), kind=kCustom, calls=%fused_computation.clone.1 | custom fusion | bytes 1574912 | tf_op jit(solution)/shard_map/while/body/eval_jaxpr/jit(_take)/gather | solution.py:56
  51.0 1.3 fusion.30
  54.3 2.4 %gather_fusion = bf16[512,3,256]{2,1,0:T(4,128)(2,1)S(1)} fusion(bf16[3,416,256]{2,0,1:T(4,128)(2,1)S(1)} %get-tuple-element.240, s32[1024]{0:T(1024)S(1)} %pad_clamp_fusion.3), kind=kCustom, calls=%fused_computation.clone.1 | custom fusion | bytes 1574912 | tf_op jit(solution)/shard_map/while/body/eval_jaxpr/jit(_take)/gather | solution.py:56
  56.7 1.3 fusion.30
  60.0 2.4 %gather_fusion = bf16[512,3,256]{2,1,0:T(4,128)(2,1)S(1)} fusion(bf16[3,416,256]{2,0,1:T(4,128)(2,1)S(1)} %get-tuple-element.240, s32[1024]{0:T(1024)S(1)} %pad_clamp_fusion.3), kind=kCustom, calls=%fused_computation.clone.1 | custom fusion | bytes 1574912 | tf_op jit(solution)/shard_map/while/body/eval_jaxpr/jit(_take)/gather | solution.py:56
  62.4 1.3 fusion.30
  65.7 2.4 %gather_fusion = bf16[512,3,256]{2,1,0:T(4,128)(2,1)S(1)} fusion(bf16[3,416,256]{2,0,1:T(4,128)(2,1)S(1)} %get-tuple-element.240, s32[1024]{0:T(1024)S(1)} %pad_clamp_fusion.3), kind=kCustom, calls=%fused_computation.clone.1 | custom fusion | bytes 1574912 | tf_op jit(solution)/shard_map/while/body/eval_jaxpr/jit(_take)/gather | solution.py:56
  68.1 1.3 fusion.30
  71.4 2.4 %gather_fusion = bf16[512,3,256]{2,1,0:T(4,128)(2,1)S(1)} fusion(bf16[3,416,256]{2,0,1:T(4,128)(2,1)S(1)} %get-tuple-element.240, s32[1024]{0:T(1024)S(1)} %pad_clamp_fusion.3), kind=kCustom, calls=%fused_computation.clone.1 | custom fusion | bytes 1574912 | tf_op jit(solution)/shard_map/while/body/eval_jaxpr/jit(_take)/gather | solution.py:56
  73.8 1.3 fusion.30
  77.1 2.4 %gather_fusion = bf16[512,3,256]{2,1,0:T(4,128)(2,1)S(1)} fusion(bf16[3,416,256]{2,0,1:T(4,128)(2,1)S(1)} %get-tuple-element.240, s32[1024]{0:T(1024)S(1)} %pad_clamp_fusion.3), kind=kCustom, calls=%fused_computation.clone.1 | custom fusion | bytes 1574912 | tf_op jit(solution)/shard_map/while/body/eval_jaxpr/jit(_take)/gather | solution.py:56
  79.5 1.3 fusion.30
  82.7 2.4 %gather_fusion = bf16[512,3,256]{2,1,0:T(4,128)(2,1)S(1)} fusion(bf16[3,416,256]{2,0,1:T(4,128)(2,1)S(1)} %get-tuple-element.240, s32[1024]{0:T(1024)S(1)} %pad_clamp_fusion.3), kind=kCustom, calls=%fused_computation.clone.1 | custom fusion | bytes 1574912 | tf_op jit(solution)/shard_map/while/body/eval_jaxpr/jit(_take)/gather | solution.py:56
  88.4 2.4 %gather_fusion = bf16[512,3,256]{2,1,0:T(4,128)(2,1)S(1)} fusion(bf16[3,416,256]{2,0,1:T(4,128)(2,1)S(1)} %get-tuple-element.240, s32[1024]{0:T(1024)S(1)} %pad_clamp_fusion.3), kind=kCustom, calls=%fused_computation.clone.1 | custom fusion | bytes 1574912 | tf_op jit(solution)/shard_map/while/body/eval_jaxpr/jit(_take)/gather | solution.py:56
  94.1 2.4 %gather_fusion = bf16[512,3,256]{2,1,0:T(4,128)(2,1)S(1)} fusion(bf16[3,416,256]{2,0,1:T(4,128)(2,1)S(1)} %get-tuple-element.240, s32[1024]{0:T(1024)S(1)} %pad_clamp_fusion.3), kind=kCustom, calls=%fused_computation.clone.1 | custom fusion | bytes 1574912 | tf_op jit(solution)/shard_map/while/body/eval_jaxpr/jit(_take)/gather | solution.py:56
  99.8 2.4 %gather_fusion = bf16[512,3,256]{2,1,0:T(4,128)(2,1)S(1)} fusion(bf16[3,416,256]{2,0,1:T(4,128)(2,1)S(1)} %get-tuple-element.240, s32[1024]{0:T(1024)S(1)} %pad_clamp_fusion.3), kind=kCustom, calls=%fused_computation.clone.1 | custom fusion | bytes 1574912 | tf_op jit(solution)/shard_map/while/body/eval_jaxpr/jit(_take)/gather | solution.py:56
  102.2 1.3 fusion.30
  105.5 2.4 %gather_fusion = bf16[512,3,256]{2,1,0:T(4,128)(2,1)S(1)} fusion(bf16[3,416,256]{2,0,1:T(4,128)(2,1)S(1)} %get-tuple-element.240, s32[1024]{0:T(1024)S(1)} %pad_clamp_fusion.3), kind=kCustom, calls=%fused_computation.clone.1 | custom fusion | bytes 1574912 | tf_op jit(solution)/shard_map/while/body/eval_jaxpr/jit(_take)/gather | solution.py:56
  111.2 2.4 %gather_fusion = bf16[512,3,256]{2,1,0:T(4,128)(2,1)S(1)} fusion(bf16[3,416,256]{2,0,1:T(4,128)(2,1)S(1)} %get-tuple-element.240, s32[1024]{0:T(1024)S(1)} %pad_clamp_fusion.3), kind=kCustom, calls=%fused_computation.clone.1 | custom fusion | bytes 1574912 | tf_op jit(solution)/shard_map/while/body/eval_jaxpr/jit(_take)/gather | solution.py:56
  116.7 66.0 %all-gather.3.cloned.1.call-done = f32[64,128,128]{2,1,0:T(8,128)} async-done(((f32[2,128,128]{2,1,0:T(8,128)}), f32[64,128,128]{2,1,0:T(8,128)}) %all-gather.3.cloned.1.call-update) | async-done | bytes 4194320 | tf_op jit(solution)/shard_map/all_gather | solution.py:8
  182.7 2.4 %reduce_sum.9 = f32[2,128,128]{2,1,0:T(8,128)S(1)} reduce(f32[32,2,128,128]{3,2,1,0:T(8,128)} %bitcast.87, f32[]{:T(128)} %constant.109.clone.1), dimensions={0}, to_apply=%region_2.3 | reduce | flops 1015808 | bytes 4325380 | tf_op jit(solution)/shard_map/reduce_sum | solution.py:9
  (136 shorter events, 48.9 us)
Async XLA Ops:
  7.2 175.5 %all-gather.3.cloned.1.call-start = ((), (), s32[]{:S(2)}) async-start(), calls=%async_computation | async-start | bytes 4325376 | tf_op jit(solution)/shard_map/all_gather | solution.py:8
  11.3 5.3 %collective-permute-start.1 = (bf16[3,1,1,32,256]{4,0,3,2,1:T(4,128)(2,1)S(1)}, bf16[3,1,1,32,256]{4,0,3,2,1:T(4,128)(2,1)S(1)}, u32[]{:S(2)}, u32[]{:S(2)}) collective-permute-start(bf16[3,1,1,32,256]{4,0,3,2,1:T(4,128)(2,1)S(1)} %bitcast_select_fusion), channel_id=1, source_target_pairs={{4,0},{8,4},{12,8},{16,12},{20,16},{24,20},{28,24},{5,1},{9,5},{13... | collective-permute-start | bytes 147464 | tf_op jit(solution)/shard_map/ppermute | solution.py:21
  12.6 4.0 %collective-permute-start = (bf16[3,1,1,32,256]{4,0,3,2,1:T(4,128)(2,1)S(1)}, bf16[3,1,1,32,256]{4,0,3,2,1:T(4,128)(2,1)S(1)}, u32[]{:S(2)}, u32[]{:S(2)}) collective-permute-start(bf16[3,1,1,32,256]{4,0,3,2,1:T(4,128)(2,1)S(1)} %bitcast_select_fusion), channel_id=1, source_target_pairs={{0,4},{4,8},{8,12},{12,16},{16,20},{20,24},{24,28},{1,5},{5,9},{9,... | collective-permute-start | bytes 147464 | tf_op jit(solution)/shard_map/ppermute | solution.py:20
  16.8 9.8 %collective-permute-start.3 = (bf16[3,3,1,32,256]{4,0,3,2,1:T(4,128)(2,1)S(1)}, bf16[3,3,1,32,256]{4,0,3,2,1:T(4,128)(2,1)S(1)}, u32[]{:S(2)}, u32[]{:S(2)}) collective-permute-start(bf16[3,3,1,32,256]{4,0,3,2,1:T(4,128)(2,1)S(1)} %pad_maximum_fusion.3), channel_id=1, source_target_pairs={{1,0},{2,1},{3,2},{5,4},{6,5},{7,6},{9,8},{10,9},{11,10},{13,12},{... | collective-permute-start | bytes 442376 | tf_op jit(solution)/shard_map/ppermute | solution.py:21
  18.1 10.2 %collective-permute-start.2 = (bf16[3,3,1,32,256]{4,0,3,2,1:T(4,128)(2,1)S(1)}, bf16[3,3,1,32,256]{4,0,3,2,1:T(4,128)(2,1)S(1)}, u32[]{:S(2)}, u32[]{:S(2)}) collective-permute-start(bf16[3,3,1,32,256]{4,0,3,2,1:T(4,128)(2,1)S(1)} %pad_maximum_fusion.3), channel_id=1, source_target_pairs={{0,1},{1,2},{2,3},{4,5},{5,6},{6,7},{8,9},{9,10},{10,11},{12,13},{... | collective-permute-start | bytes 442376 | tf_op jit(solution)/shard_map/ppermute | solution.py:20
  29.5 85.5 %copy-start = (bf16[3,128,128]{2,1,0:T(8,128)(2,1)S(1)}, bf16[3,128,128]{2,1,0:T(8,128)(2,1)}, u32[]{:S(2)}) copy-start(bf16[3,128,128]{2,1,0:T(8,128)(2,1)} %param.9) | copy-start | bytes 294916
  185.1 1.4 copy-start.1
Sparse Core Ops, SparseCore 0:
  116.8 65.8 all-gather.2
